TPU v7x, 32 devices: a whole 2x2x4 slice. The times are simulated.
32 devices in a mesh: group: 2 (over x), expert: 16 (over z, y, core).
Axes of the slice: x: 2, y: 2, z: 4, core: 2. Of those that a mesh axis runs over, the one named last changes fastest.
Arguments:
- tokens: bfloat16 [128, 7168], P(('group', 'expert')), parts along dimension 0, may hold values from -6 to 6
- expert_ids: int32 [128, 2], P(('group', 'expert')), parts along dimension 0, may hold values from 0 to 1, all different within a row; in each aligned block of 4 rows (0 to 3, 4 to 7, ...) at most 4 rows name the same one
- gate_codes: int32 [128, 2], P(('group', 'expert')), parts along dimension 0, may hold values from 1 to 65535
- gate_weight: bfloat16 [16, 7168, 256], P('expert'), may hold values from -0.0625 to 0.0625
- up_weight: bfloat16 [16, 7168, 256], P('expert'), may hold values from -0.0625 to 0.0625
- down_weight: bfloat16 [16, 256, 7168], P('expert'), may hold values from -0.125 to 0.125
- target_basis: bfloat16 [7168, 512], P('expert'), may hold values from -0.0625 to 0.0625
Outputs:
- targets: bfloat16 [128, 512], P(('group', 'expert')), parts along dimension 0
There are 2 independent parts, one for each index of `group`. A program takes and returns all parts, laid end to end along the dimension named above; an argument that names none is the same for every part. Nothing has to cross between parts.
Inputs may be any that keep to these rules, and one draw needn't show every extreme that they name: `expert_ids`: each row names 2 different experts; among the 4 rows of one device no expert is named more than 4 times, a bound that some block reaches.
All inputs are finite; a program needn't handle non-finite values.
Results may differ from a plain program's by a relative error of at most 0.0057.
Values may be sent and summed in bfloat16 or wider, within the bound.
No kernel may reach another device: no remote copies, remote signals or barrier semaphores. Data moves between devices by JAX's collectives and lax.ppermute only.
A program may use at most 128 MiB of HBM per device.

v0:
```python
import jax
import jax.numpy as jnp
from jax import lax
from jax.sharding import PartitionSpec as P

SLICES = 8


def run_expert(received, gate_weight, up_weight, down_weight):
    sources, slots, feature_width = received.shape
    row_block = received.reshape(sources * slots, feature_width)
    gate_act = jnp.dot(row_block, gate_weight[0], preferred_element_type=jnp.float32)
    up_act = jnp.dot(row_block, up_weight[0], preferred_element_type=jnp.float32)
    hidden = (jax.nn.silu(gate_act) * up_act).astype(jnp.bfloat16)
    expert_part = jnp.dot(hidden, down_weight[0], preferred_element_type=jnp.float32).astype(
        jnp.bfloat16
    )
    return expert_part.reshape(sources, slots, feature_width)


def shards(tokens, expert_ids, gate_codes, gate_weight, up_weight, down_weight, target_basis):
    token_count, feature_width = tokens.shape
    pick_count = expert_ids.shape[1]
    owner_count = lax.axis_size("expert")
    expert_count = owner_count // SLICES
    capacity = min(token_count, max(2, 5 * token_count * pick_count // (4 * expert_count)))
    rank_width = target_basis.shape[1]
    flat_ids = expert_ids.reshape(-1)
    onehot = (flat_ids[:, None] == jnp.arange(expert_count, dtype=jnp.int32)[None, :]).astype(
        jnp.int32
    )
    before = jnp.cumsum(onehot, axis=0) - onehot
    slot_rank = jnp.sum(before * onehot, axis=1)
    slot_index = flat_ids * capacity + slot_rank
    row_token = jnp.arange(token_count * pick_count, dtype=jnp.int32) // pick_count
    slot_table = (
        jnp.full((expert_count * capacity,), token_count, jnp.int32).at[slot_index].set(row_token)
    )
    padded = jnp.concatenate([tokens, jnp.zeros((1, feature_width), tokens.dtype)], axis=0)
    per_expert_rows = padded[slot_table].reshape(expert_count, 1, capacity, feature_width)
    outgoing = jnp.broadcast_to(per_expert_rows, (expert_count, SLICES, capacity, feature_width))
    outgoing = outgoing.reshape(owner_count, capacity, feature_width)
    full_basis = lax.all_gather(target_basis, "expert", axis=0, tiled=True)
    expert_part = run_expert(
        lax.all_to_all(outgoing, "expert", split_axis=0, concat_axis=0, tiled=True),
        gate_weight,
        up_weight,
        down_weight,
    )
    result = jnp.einsum("skd,dr->skr", expert_part, full_basis, preferred_element_type=jnp.float32)
    returned = lax.all_to_all(result, "expert", split_axis=0, concat_axis=0, tiled=True)
    summed = jnp.sum(returned.reshape(expert_count, SLICES, capacity, rank_width), axis=1)
    projected = summed.reshape(expert_count * capacity, rank_width)[slot_index]
    codes_float = gate_codes.astype(jnp.float32)
    weights = 2.5 * codes_float / jnp.sum(codes_float, axis=1, keepdims=True)
    projected = projected.reshape(token_count, pick_count, rank_width)
    return jnp.sum(weights[:, :, None] * projected, axis=1).astype(jnp.bfloat16)


def solution(mesh):
    in_specs = (
        P(("group", "expert"), None),
        P(("group", "expert"), None),
        P(("group", "expert"), None),
        P("expert", None, None),
        P("expert", None, None),
        P("expert", None, None),
        P("expert", None),
    )
    out_specs = P(("group", "expert"), None)
    return jax.shard_map(shards, mesh=mesh, in_specs=in_specs, out_specs=out_specs, check_vma=False)
```

profile of v0, /device:TPU:0, one launch (start us, length us, event | category | flops | bytes accessed | tf_op | source)
XLA Modules:
  0.0 121.8 jit_solution(8186890199680378276)
XLA Ops:
  6.5 0.0 copy-start
  6.5 0.0 all-gather.2.cloned.1.call-start
  6.5 0.7 all-gather.2.cloned.1.call-update
  7.3 0.8 copy.25
  8.0 0.1 eq.15
  8.1 0.7 broadcast_multiply_fusion
  8.8 0.1 copy.24
  8.9 0.1 mul.37
  9.0 0.2 reduce_window_sum.11
  9.2 0.8 concatenate.3
  10.1 0.6 scatter_custom_fusion
  10.7 0.6 gather_fusion
  11.3 0.1 broadcast_in_dim.7
  11.4 1.2 broadcast_in_dim.8
  12.5 7.4 %all-to-all-start = ((bf16[16,4,7168]{2,1,0:T(4,128)(2,1)}), bf16[16,4,7168]{2,1,0:T(4,128)(2,1)S(1)}, u32[]{:S(2)}, u32[]{:S(2)}) async-start(bf16[16,4,7168]{2,1,0:T(4,128)(2,1)} %bitcast.2), calls=%async_computation | async-start | bytes 1835008 | tf_op jit(solution)/shard_map/all_to_all | solution.py:45
  19.9 0.0 copy-done
  20.0 35.1 %all-to-all-done = bf16[16,4,7168]{2,1,0:T(4,128)(2,1)S(1)} async-done(((bf16[16,4,7168]{2,1,0:T(4,128)(2,1)}), bf16[16,4,7168]{2,1,0:T(4,128)(2,1)S(1)}, u32[]{:S(2)}, u32[]{:S(2)}) %all-to-all-start) | async-done | bytes 917536 | tf_op jit(solution)/shard_map/all_to_all | solution.py:45
  55.1 0.2 reshape.53
  55.3 2.8 %fusion.5 = f32[64,256]{1,0:T(8,128)S(1)} fusion(bf16[64,7168]{1,0:T(8,128)(2,1)S(1)} %reshape.53, bf16[1,7168,256]{2,1,0:T(8,128)(2,1)} %param.10), kind=kOutput, calls=%fused_computation.9 | convolution fusion | flops 234881024 | bytes 4653056 | tf_op jit(solution)/shard_map/dot_general | solution.py:12
  58.0 5.5 %convolution_convert_fusion = bf16[64,7168]{1,0:T(8,128)(2,1)S(1)} fusion(bf16[1,256,7168]{2,1,0:T(8,128)(2,1)} %param.12, bf16[64,7168]{1,0:T(8,128)(2,1)S(1)} %reshape.53, bf16[1,7168,256]{2,1,0:T(8,128)(2,1)} %param.11, f32[64,256]{1,0:T(8,128)S(1)} %fusion.5), kind=kOutput, calls=%fused_computation.3 | convolution fusion | flops 470319104 | bytes 9240576 | tf_op jit(solution)/shard_map/dot_general | solution.py:15
  63.5 0.3 reshape.54
  63.8 33.4 %all-gather.2.cloned.1.call-done = bf16[7168,512]{1,0:T(8,128)(2,1)} async-done(((bf16[448,512]{1,0:T(8,128)(2,1)}), bf16[7168,512]{1,0:T(8,128)(2,1)}) %all-gather.2.cloned.1.call-update) | async-done | bytes 7340048 | tf_op jit(solution)/shard_map/all_gather | solution.py:43
  97.3 4.2 %fusion = f32[16,4,512]{2,0,1:T(8,128)S(1)} fusion(bf16[7168,512]{1,0:T(8,128)(2,1)} %all-gather.2.cloned.1.call-done, bf16[16,4,7168]{2,1,0:T(4,128)(2,1)S(1)} %reshape.54), kind=kOutput, calls=%fused_computation.4 | convolution fusion | flops 469762048 | bytes 8388608 | tf_op jit(solution)/shard_map/skd,dr->skr/dot_general | solution.py:50
  101.5 0.7 copy.27
  102.2 3.5 %all-to-all-start.1 = ((f32[16,4,512]{2,1,0:T(4,128)}), f32[16,4,512]{2,1,0:T(4,128)S(1)}, u32[]{:S(2)}, u32[]{:S(2)}) async-start(f32[16,4,512]{2,1,0:T(4,128)} %copy.27), calls=%async_computation.1 | async-start | bytes 262144 | tf_op jit(solution)/shard_map/all_to_all | solution.py:51
  105.8 0.1 copy.23
  105.9 7.8 %all-to-all-done.1 = f32[16,4,512]{2,1,0:T(4,128)S(1)} async-done(((f32[16,4,512]{2,1,0:T(4,128)}), f32[16,4,512]{2,1,0:T(4,128)S(1)}, u32[]{:S(2)}, u32[]{:S(2)}) %all-to-all-start.1) | async-done | bytes 131104 | tf_op jit(solution)/shard_map/all_to_all | solution.py:51
  113.7 0.6 gather_fusion.1
  114.2 0.7 multiply_reduce_fusion
  (12 shorter events, 0.1 us)
Async XLA Ops:
  6.5 13.4 %copy-start = (s32[4,2]{0,1:T(2,128)S(1)}, s32[4,2]{0,1:T(2,128)}, u32[]{:S(2)}) copy-start(s32[4,2]{0,1:T(2,128)} %param.9) | copy-start | bytes 100
  6.5 90.7 %all-gather.2.cloned.1.call-start = ((), (), s32[]{:S(2)}) async-start(), calls=%async_computation.2 | async-start | bytes 7798784 | tf_op jit(solution)/shard_map/all_gather | solution.py:43
  12.5 42.5 %all-to-all-start = ((bf16[16,4,7168]{2,1,0:T(4,128)(2,1)}), bf16[16,4,7168]{2,1,0:T(4,128)(2,1)S(1)}, u32[]{:S(2)}, u32[]{:S(2)}) async-start(bf16[16,4,7168]{2,1,0:T(4,128)(2,1)} %bitcast.2), calls=%async_computation | async-start | bytes 1835008 | tf_op jit(solution)/shard_map/all_to_all | solution.py:45
  102.2 11.4 %all-to-all-start.1 = ((f32[16,4,512]{2,1,0:T(4,128)}), f32[16,4,512]{2,1,0:T(4,128)S(1)}, u32[]{:S(2)}, u32[]{:S(2)}) async-start(f32[16,4,512]{2,1,0:T(4,128)} %copy.27), calls=%async_computation.1 | async-start | bytes 262144 | tf_op jit(solution)/shard_map/all_to_all | solution.py:51
Sparse Core Ops, SparseCore 0:
  9.6 87.5 all-gather.1
where the time goes:
time: 122 us
  waiting for transfers between devices  77 us (63%)
  between operations  13.5 us (11%)
  matrix products  12.4 us (10%)
  starting transfers between devices  10.9 us (9%)
  local copies, waits for them, and re-layouts  6.25 us (5%)
  other arithmetic  1.66 us (1%)
    all_to_all x1, waiting for transfers between devices, shards(): lax.all_to_all(outgoing, 'expert', split_axis=0, concat_axis=0, tiled=True)  35.1 us
    all_gather x1, waiting for transfers between devices, shards(): full_basis = lax.all_gather(target_basis, 'expert', axis=0, tiled=True)  33.4 us
    all_to_all x1, waiting for transfers between devices, shards(): lax.all_to_all(result, 'expert', split_axis=0, concat_axis=0, tiled=True)  7.76 us
    all_to_all x1, starting transfers between devices, shards(): lax.all_to_all(outgoing, 'expert', split_axis=0, concat_axis=0, tiled=True)  7.41 us
    dot_general x1, matrix products, run_expert(): jnp.dot(hidden, down_weight[0], preferred_element_type=jnp.float32)  5.45 us
    dot_general x1, matrix products, shards(): jnp.einsum('skd,dr->skr', expert_part, full_basis, preferred_element_type...  4.23 us
    all_to_all x1, starting transfers between devices, shards(): lax.all_to_all(result, 'expert', split_axis=0, concat_axis=0, tiled=True)  3.51 us
    dot_general x1, matrix products, run_expert(): jnp.dot(row_block, gate_weight[0], preferred_element_type=jnp.float32)  2.76 us
  transfers between devices with their start and end apart: 3, of which 3 were waited for; matrix products, arithmetic and copies ran while one was open for 12% of the time, Pallas kernels for 0%

commit v1 on v0

--- a/solution.py
+++ b/solution.py
@@ -1,9 +1,29 @@
+import functools
 import jax
 import jax.numpy as jnp
 from jax import lax
 from jax.sharding import PartitionSpec as P
 
 SLICES = 8
+
+
+def plan_matrix(z, array_axis):
+    workers = lax.axis_size("expert")
+    carry = range(workers)
+    k_now = map(lambda h: (h, (h + 1) % workers), carry)
+    seen = list(k_now)
+
+    def fill_zones(local_part):
+        if len(local_part) == workers:
+            return local_part
+        carry_in = lax.ppermute(local_part[0], "expert", seen)
+        return fill_zones([carry_in, *local_part])
+
+    r_now = jnp.concatenate(fill_zones([z]), axis=array_axis)
+    return jnp.roll(r_now, (lax.axis_index("expert") + 1) * z.shape[array_axis], array_axis)
+
+
+drive_table = functools.partial(plan_matrix, array_axis=0)
 
 
 def run_expert(received, gate_weight, up_weight, down_weight):
@@ -40,7 +60,7 @@
     per_expert_rows = padded[slot_table].reshape(expert_count, 1, capacity, feature_width)
     outgoing = jnp.broadcast_to(per_expert_rows, (expert_count, SLICES, capacity, feature_width))
     outgoing = outgoing.reshape(owner_count, capacity, feature_width)
-    full_basis = lax.all_gather(target_basis, "expert", axis=0, tiled=True)
+    full_basis = drive_table(target_basis)
     expert_part = run_expert(
         lax.all_to_all(outgoing, "expert", split_axis=0, concat_axis=0, tiled=True),
         gate_weight,

time: 122 us -> 212 us (1.74)
  waiting for transfers between devices: 77 us -> 160 us
  local copies, waits for them, and re-layouts: 6.25 us -> 28.6 us
  between operations: 13.5 us -> 0.53 us
    ppermute x0 -> x15, waiting for transfers between devices: none -> 152 us  [fill_zones(): carry_in = lax.ppermute(local_part[0], 'expert', seen)]
    all_to_all x1, waiting for transfers between devices: 35.1 us -> 0.01 us  [shards(): lax.all_to_all(outgoing, 'expert', split_axis=0, concat_axis=0, tiled=True)]
    all_gather x1 -> x0, waiting for transfers between devices: 33.4 us -> none  [shards(): full_basis = lax.all_gather(target_basis, 'expert', axis=0, tiled=True)]
    unnamed x3 -> x80, local copies, waits for them, and re-layouts: 0.77 us -> 23.1 us
    dot_general x1, matrix products: 4.23 us -> 2.06 us  [shards(): jnp.einsum('skd,dr->skr', expert_part, full_basis, preferred_element_type...]
  transfers between devices with their start and end apart: 3 -> 17, of which waited for: 3 -> 16; matrix products, arithmetic and copies ran while one was open for 12% -> 7% of each run, Pallas kernels for 0% -> 0%
where the time goes in v1:
time: 212 us; the launch traced here: 211 us
  waiting for transfers between devices  160 us (75%)
  local copies, waits for them, and re-layouts  28.6 us (13%)
  matrix products  10.3 us (5%)
  starting transfers between devices  9.85 us (5%)
  other arithmetic  2.33 us (1%)
    ppermute x15, waiting for transfers between devices, fill_zones(): carry_in = lax.ppermute(local_part[0], 'expert', seen)  152 us
    unnamed x80, local copies, waits for them, and re-layouts  23.1 us
    all_to_all x1, waiting for transfers between devices, shards(): lax.all_to_all(result, 'expert', split_axis=0, concat_axis=0, tiled=True)  7.75 us
    all_to_all x1, starting transfers between devices, shards(): lax.all_to_all(outgoing, 'expert', split_axis=0, concat_axis=0, tiled=True)  5.81 us
    dot_general x1, matrix products, run_expert(): jnp.dot(hidden, down_weight[0], preferred_element_type=jnp.float32)  5.45 us
  transfers between devices with their start and end apart: 17, of which 16 were waited for; matrix products, arithmetic and copies ran while one was open for 7% of the time, Pallas kernels for 0%

profile of v1, /device:TPU:0, one launch (start us, length us, event | category | flops | bytes accessed | tf_op | source)
XLA Modules:
  0.0 211.3 jit_solution(14295122072014855219)
XLA Ops:
  0.5 11.4 %collective-permute-done = bf16[448,512]{1,0:T(8,128)(2,1)S(1)} collective-permute-done((bf16[448,512]{1,0:T(8,128)(2,1)}, bf16[448,512]{1,0:T(8,128)(2,1)S(1)}, u32[]{:S(2)}, u32[]{:S(2)}) %collective-permute-start) | collective-permute-done | bytes 458784 | tf_op jit(solution)/shard_map/ppermute | solution.py:19
  11.8 10.6 %collective-permute-done.1 = bf16[448,512]{1,0:T(8,128)(2,1)S(1)} collective-permute-done((bf16[448,512]{1,0:T(8,128)(2,1)S(1)}, bf16[448,512]{1,0:T(8,128)(2,1)S(1)}, u32[]{:S(2)}, u32[]{:S(2)}) %collective-permute-start.1) | collective-permute-done | bytes 458784 | tf_op jit(solution)/shard_map/ppermute | solution.py:19
  23.3 10.6 %collective-permute-done.2 = bf16[448,512]{1,0:T(8,128)(2,1)S(1)} collective-permute-done((bf16[448,512]{1,0:T(8,128)(2,1)S(1)}, bf16[448,512]{1,0:T(8,128)(2,1)S(1)}, u32[]{:S(2)}, u32[]{:S(2)}) %collective-permute-start.2) | collective-permute-done | bytes 458784 | tf_op jit(solution)/shard_map/ppermute | solution.py:19
  34.6 10.6 %collective-permute-done.3 = bf16[448,512]{1,0:T(8,128)(2,1)S(1)} collective-permute-done((bf16[448,512]{1,0:T(8,128)(2,1)S(1)}, bf16[448,512]{1,0:T(8,128)(2,1)S(1)}, u32[]{:S(2)}, u32[]{:S(2)}) %collective-permute-start.3) | collective-permute-done | bytes 458784 | tf_op jit(solution)/shard_map/ppermute | solution.py:19
  46.0 10.6 %collective-permute-done.4 = bf16[448,512]{1,0:T(8,128)(2,1)S(1)} collective-permute-done((bf16[448,512]{1,0:T(8,128)(2,1)S(1)}, bf16[448,512]{1,0:T(8,128)(2,1)S(1)}, u32[]{:S(2)}, u32[]{:S(2)}) %collective-permute-start.4) | collective-permute-done | bytes 458784 | tf_op jit(solution)/shard_map/ppermute | solution.py:19
  57.4 10.6 %collective-permute-done.5 = bf16[448,512]{1,0:T(8,128)(2,1)S(1)} collective-permute-done((bf16[448,512]{1,0:T(8,128)(2,1)S(1)}, bf16[448,512]{1,0:T(8,128)(2,1)S(1)}, u32[]{:S(2)}, u32[]{:S(2)}) %collective-permute-start.5) | collective-permute-done | bytes 458784 | tf_op jit(solution)/shard_map/ppermute | solution.py:19
  68.8 10.6 %collective-permute-done.6 = bf16[448,512]{1,0:T(8,128)(2,1)S(1)} collective-permute-done((bf16[448,512]{1,0:T(8,128)(2,1)S(1)}, bf16[448,512]{1,0:T(8,128)(2,1)S(1)}, u32[]{:S(2)}, u32[]{:S(2)}) %collective-permute-start.6) | collective-permute-done | bytes 458784 | tf_op jit(solution)/shard_map/ppermute | solution.py:19
  80.9 9.1 %collective-permute-done.7 = bf16[448,512]{1,0:T(8,128)(2,1)S(1)} collective-permute-done((bf16[448,512]{1,0:T(8,128)(2,1)S(1)}, bf16[448,512]{1,0:T(8,128)(2,1)S(1)}, u32[]{:S(2)}, u32[]{:S(2)}) %collective-permute-start.7) | collective-permute-done | bytes 458784 | tf_op jit(solution)/shard_map/ppermute | solution.py:19
  91.9 8.7 %collective-permute-done.8 = bf16[448,512]{1,0:T(8,128)(2,1)S(1)} collective-permute-done((bf16[448,512]{1,0:T(8,128)(2,1)S(1)}, bf16[448,512]{1,0:T(8,128)(2,1)S(1)}, u32[]{:S(2)}, u32[]{:S(2)}) %collective-permute-start.8) | collective-permute-done | bytes 458784 | tf_op jit(solution)/shard_map/ppermute | solution.py:19
  101.3 1.2 broadcast_in_dim.8
  102.5 5.8 %all-to-all-start = ((bf16[16,4,7168]{2,1,0:T(4,128)(2,1)}), bf16[16,4,7168]{2,1,0:T(4,128)(2,1)S(1)}, u32[]{:S(2)}, u32[]{:S(2)}) async-start(bf16[16,4,7168]{2,1,0:T(4,128)(2,1)} %bitcast.2), calls=%async_computation | async-start | bytes 1835008 | tf_op jit(solution)/shard_map/all_to_all | solution.py:65
  108.3 2.9 %collective-permute-done.9 = bf16[448,512]{1,0:T(8,128)(2,1)S(1)} collective-permute-done((bf16[448,512]{1,0:T(8,128)(2,1)S(1)}, bf16[448,512]{1,0:T(8,128)(2,1)S(1)}, u32[]{:S(2)}, u32[]{:S(2)}) %collective-permute-start.9) | collective-permute-done | bytes 458784 | tf_op jit(solution)/shard_map/ppermute | solution.py:19
  111.2 22.8 %collective-permute-done.10 = bf16[448,512]{1,0:T(8,128)(2,1)S(1)} collective-permute-done((bf16[448,512]{1,0:T(8,128)(2,1)S(1)}, bf16[448,512]{1,0:T(8,128)(2,1)S(1)}, u32[]{:S(2)}, u32[]{:S(2)}) %collective-permute-start.10) | collective-permute-done | bytes 458784 | tf_op jit(solution)/shard_map/ppermute | solution.py:19
  134.0 10.6 %collective-permute-done.11 = bf16[448,512]{1,0:T(8,128)(2,1)S(1)} collective-permute-done((bf16[448,512]{1,0:T(8,128)(2,1)S(1)}, bf16[448,512]{1,0:T(8,128)(2,1)S(1)}, u32[]{:S(2)}, u32[]{:S(2)}) %collective-permute-start.11) | collective-permute-done | bytes 458784 | tf_op jit(solution)/shard_map/ppermute | solution.py:19
  144.6 10.7 %collective-permute-done.12 = bf16[448,512]{1,0:T(8,128)(2,1)} collective-permute-done((bf16[448,512]{1,0:T(8,128)(2,1)S(1)}, bf16[448,512]{1,0:T(8,128)(2,1)}, u32[]{:S(2)}, u32[]{:S(2)}) %collective-permute-start.12) | collective-permute-done | bytes 458784 | tf_op jit(solution)/shard_map/ppermute | solution.py:19
  156.2 2.8 %fusion.6 = f32[64,256]{1,0:T(8,128)S(1)} fusion(bf16[64,7168]{1,0:T(8,128)(2,1)S(1)} %reshape.53, bf16[1,7168,256]{2,1,0:T(8,128)(2,1)} %param.10), kind=kOutput, calls=%fused_computation.10 | convolution fusion | flops 234881024 | bytes 4653056 | tf_op jit(solution)/shard_map/dot_general | solution.py:32
  159.1 7.2 %collective-permute-done.13 = bf16[448,512]{1,0:T(8,128)(2,1)} collective-permute-done((bf16[448,512]{1,0:T(8,128)(2,1)}, bf16[448,512]{1,0:T(8,128)(2,1)}, u32[]{:S(2)}, u32[]{:S(2)}) %collective-permute-start.13) | collective-permute-done | bytes 458784 | tf_op jit(solution)/shard_map/ppermute | solution.py:19
  166.2 5.5 %convolution_convert_fusion = bf16[64,7168]{1,0:T(8,128)(2,1)S(1)} fusion(bf16[1,256,7168]{2,1,0:T(8,128)(2,1)} %param.12, bf16[64,7168]{1,0:T(8,128)(2,1)S(1)} %reshape.53, bf16[1,7168,256]{2,1,0:T(8,128)(2,1)} %param.11, f32[64,256]{1,0:T(8,128)S(1)} %fusion.6), kind=kOutput, calls=%fused_computation.3 | convolution fusion | flops 470319104 | bytes 9240576 | tf_op jit(solution)/shard_map/dot_general | solution.py:35
  172.1 5.0 %collective-permute-done.14 = bf16[448,512]{1,0:T(8,128)(2,1)} collective-permute-done((bf16[448,512]{1,0:T(8,128)(2,1)}, bf16[448,512]{1,0:T(8,128)(2,1)}, u32[]{:S(2)}, u32[]{:S(2)}) %collective-permute-start.14) | collective-permute-done | bytes 458784 | tf_op jit(solution)/shard_map/ppermute | solution.py:19
  178.2 1.1 constant_dynamic-update-slice_fusion.30
  179.2 1.1 constant_dynamic-update-slice_fusion.29
  180.3 1.1 constant_dynamic-update-slice_fusion.28
  181.4 1.1 constant_dynamic-update-slice_fusion.27
  182.4 1.1 constant_dynamic-update-slice_fusion.26
  183.5 1.1 constant_dynamic-update-slice_fusion.25
  184.5 1.1 constant_dynamic-update-slice_fusion.24
  185.6 1.1 constant_dynamic-update-slice_fusion.23
  186.6 1.1 constant_dynamic-update-slice_fusion.22
  187.7 1.1 constant_dynamic-update-slice_fusion.21
  195.8 2.1 fusion
  198.6 3.5 %all-to-all-start.1 = ((f32[16,4,512]{2,1,0:T(4,128)}), f32[16,4,512]{2,1,0:T(4,128)S(1)}, u32[]{:S(2)}, u32[]{:S(2)}) async-start(f32[16,4,512]{2,1,0:T(4,128)} %copy.27), calls=%async_computation.1 | async-start | bytes 262144 | tf_op jit(solution)/shard_map/all_to_all | solution.py:71
  202.2 7.7 %all-to-all-done.1 = f32[16,4,512]{2,1,0:T(4,128)S(1)} async-done(((f32[16,4,512]{2,1,0:T(4,128)}), f32[16,4,512]{2,1,0:T(4,128)S(1)}, u32[]{:S(2)}, u32[]{:S(2)}) %all-to-all-start.1) | async-done | bytes 131104 | tf_op jit(solution)/shard_map/all_to_all | solution.py:71
  (114 shorter events, 19.8 us)
Async XLA Ops:
  0.0 11.8 %collective-permute-start = (bf16[448,512]{1,0:T(8,128)(2,1)}, bf16[448,512]{1,0:T(8,128)(2,1)S(1)}, u32[]{:S(2)}, u32[]{:S(2)}) collective-permute-start(bf16[448,512]{1,0:T(8,128)(2,1)} %param.13), channel_id=1, source_target_pairs={{0,1},{1,2},{2,3},{3,4},{4,5},{5,6},{6,7},{7,8},{8,9},{9,10},{10,1... | collective-permute-start | bytes 1376264 | tf_op jit(solution)/shard_map/ppermute | solution.py:19
  11.8 10.6 %collective-permute-start.1 = (bf16[448,512]{1,0:T(8,128)(2,1)S(1)}, bf16[448,512]{1,0:T(8,128)(2,1)S(1)}, u32[]{:S(2)}, u32[]{:S(2)}) collective-permute-start(bf16[448,512]{1,0:T(8,128)(2,1)S(1)} %collective-permute-done), channel_id=1, source_target_pairs={{0,1},{1,2},{2,3},{3,4},{4,5},{5,6},{6,7},{7,8},{8,9},{9,10},{10,1... | collective-permute-start | bytes 1376264 | tf_op jit(solution)/shard_map/ppermute | solution.py:19
  23.3 10.6 %collective-permute-start.2 = (bf16[448,512]{1,0:T(8,128)(2,1)S(1)}, bf16[448,512]{1,0:T(8,128)(2,1)S(1)}, u32[]{:S(2)}, u32[]{:S(2)}) collective-permute-start(bf16[448,512]{1,0:T(8,128)(2,1)S(1)} %collective-permute-done.1), channel_id=1, source_target_pairs={{0,1},{1,2},{2,3},{3,4},{4,5},{5,6},{6,7},{7,8},{8,9},{9,10},{10,1... | collective-permute-start | bytes 1376264 | tf_op jit(solution)/shard_map/ppermute | solution.py:19
  34.6 10.6 %collective-permute-start.3 = (bf16[448,512]{1,0:T(8,128)(2,1)S(1)}, bf16[448,512]{1,0:T(8,128)(2,1)S(1)}, u32[]{:S(2)}, u32[]{:S(2)}) collective-permute-start(bf16[448,512]{1,0:T(8,128)(2,1)S(1)} %collective-permute-done.2), channel_id=1, source_target_pairs={{0,1},{1,2},{2,3},{3,4},{4,5},{5,6},{6,7},{7,8},{8,9},{9,10},{10,1... | collective-permute-start | bytes 1376264 | tf_op jit(solution)/shard_map/ppermute | solution.py:19
  46.0 10.6 %collective-permute-start.4 = (bf16[448,512]{1,0:T(8,128)(2,1)S(1)}, bf16[448,512]{1,0:T(8,128)(2,1)S(1)}, u32[]{:S(2)}, u32[]{:S(2)}) collective-permute-start(bf16[448,512]{1,0:T(8,128)(2,1)S(1)} %collective-permute-done.3), channel_id=1, source_target_pairs={{0,1},{1,2},{2,3},{3,4},{4,5},{5,6},{6,7},{7,8},{8,9},{9,10},{10,1... | collective-permute-start | bytes 1376264 | tf_op jit(solution)/shard_map/ppermute | solution.py:19
  57.4 10.6 %collective-permute-start.5 = (bf16[448,512]{1,0:T(8,128)(2,1)S(1)}, bf16[448,512]{1,0:T(8,128)(2,1)S(1)}, u32[]{:S(2)}, u32[]{:S(2)}) collective-permute-start(bf16[448,512]{1,0:T(8,128)(2,1)S(1)} %collective-permute-done.4), channel_id=1, source_target_pairs={{0,1},{1,2},{2,3},{3,4},{4,5},{5,6},{6,7},{7,8},{8,9},{9,10},{10,1... | collective-permute-start | bytes 1376264 | tf_op jit(solution)/shard_map/ppermute | solution.py:19
  68.8 10.6 %collective-permute-start.6 = (bf16[448,512]{1,0:T(8,128)(2,1)S(1)}, bf16[448,512]{1,0:T(8,128)(2,1)S(1)}, u32[]{:S(2)}, u32[]{:S(2)}) collective-permute-start(bf16[448,512]{1,0:T(8,128)(2,1)S(1)} %collective-permute-done.5), channel_id=1, source_target_pairs={{0,1},{1,2},{2,3},{3,4},{4,5},{5,6},{6,7},{7,8},{8,9},{9,10},{10,1... | collective-permute-start | bytes 1376264 | tf_op jit(solution)/shard_map/ppermute | solution.py:19
  79.4 10.6 %collective-permute-start.7 = (bf16[448,512]{1,0:T(8,128)(2,1)S(1)}, bf16[448,512]{1,0:T(8,128)(2,1)S(1)}, u32[]{:S(2)}, u32[]{:S(2)}) collective-permute-start(bf16[448,512]{1,0:T(8,128)(2,1)S(1)} %collective-permute-done.6), channel_id=1, source_target_pairs={{0,1},{1,2},{2,3},{3,4},{4,5},{5,6},{6,7},{7,8},{8,9},{9,10},{10,1... | collective-permute-start | bytes 1376264 | tf_op jit(solution)/shard_map/ppermute | solution.py:19
  90.0 10.6 %collective-permute-start.8 = (bf16[448,512]{1,0:T(8,128)(2,1)S(1)}, bf16[448,512]{1,0:T(8,128)(2,1)S(1)}, u32[]{:S(2)}, u32[]{:S(2)}) collective-permute-start(bf16[448,512]{1,0:T(8,128)(2,1)S(1)} %collective-permute-done.7), channel_id=1, source_target_pairs={{0,1},{1,2},{2,3},{3,4},{4,5},{5,6},{6,7},{7,8},{8,9},{9,10},{10,1... | collective-permute-start | bytes 1376264 | tf_op jit(solution)/shard_map/ppermute | solution.py:19
  100.6 55.4 %copy-start.15 = (bf16[448,512]{1,0:T(8,128)(2,1)}, bf16[448,512]{1,0:T(8,128)(2,1)S(1)}, u32[]{:S(2)}) copy-start(bf16[448,512]{1,0:T(8,128)(2,1)S(1)} %collective-permute-done.8) | copy-start | bytes 1376260
  100.6 10.6 %collective-permute-start.9 = (bf16[448,512]{1,0:T(8,128)(2,1)S(1)}, bf16[448,512]{1,0:T(8,128)(2,1)S(1)}, u32[]{:S(2)}, u32[]{:S(2)}) collective-permute-start(bf16[448,512]{1,0:T(8,128)(2,1)S(1)} %collective-permute-done.8), channel_id=1, source_target_pairs={{0,1},{1,2},{2,3},{3,4},{4,5},{5,6},{6,7},{7,8},{8,9},{9,10},{10,1... | collective-permute-start | bytes 1376264 | tf_op jit(solution)/shard_map/ppermute | solution.py:19
  102.5 53.5 %all-to-all-start = ((bf16[16,4,7168]{2,1,0:T(4,128)(2,1)}), bf16[16,4,7168]{2,1,0:T(4,128)(2,1)S(1)}, u32[]{:S(2)}, u32[]{:S(2)}) async-start(bf16[16,4,7168]{2,1,0:T(4,128)(2,1)} %bitcast.2), calls=%async_computation | async-start | bytes 1835008 | tf_op jit(solution)/shard_map/all_to_all | solution.py:65
  111.2 44.8 %copy-start.17 = (bf16[448,512]{1,0:T(8,128)(2,1)}, bf16[448,512]{1,0:T(8,128)(2,1)S(1)}, u32[]{:S(2)}) copy-start(bf16[448,512]{1,0:T(8,128)(2,1)S(1)} %collective-permute-done.9) | copy-start | bytes 1376260
  111.2 22.8 %collective-permute-start.10 = (bf16[448,512]{1,0:T(8,128)(2,1)S(1)}, bf16[448,512]{1,0:T(8,128)(2,1)S(1)}, u32[]{:S(2)}, u32[]{:S(2)}) collective-permute-start(bf16[448,512]{1,0:T(8,128)(2,1)S(1)} %collective-permute-done.9), channel_id=1, source_target_pairs={{0,1},{1,2},{2,3},{3,4},{4,5},{5,6},{6,7},{7,8},{8,9},{9,10},{10,1... | collective-permute-start | bytes 1376264 | tf_op jit(solution)/shard_map/ppermute | solution.py:19
  134.0 32.2 %copy-start.19 = (bf16[448,512]{1,0:T(8,128)(2,1)}, bf16[448,512]{1,0:T(8,128)(2,1)S(1)}, u32[]{:S(2)}) copy-start(bf16[448,512]{1,0:T(8,128)(2,1)S(1)} %collective-permute-done.10) | copy-start | bytes 1376260
  134.0 10.6 %collective-permute-start.11 = (bf16[448,512]{1,0:T(8,128)(2,1)S(1)}, bf16[448,512]{1,0:T(8,128)(2,1)S(1)}, u32[]{:S(2)}, u32[]{:S(2)}) collective-permute-start(bf16[448,512]{1,0:T(8,128)(2,1)S(1)} %collective-permute-done.10), channel_id=1, source_target_pairs={{0,1},{1,2},{2,3},{3,4},{4,5},{5,6},{6,7},{7,8},{8,9},{9,10},{10,1... | collective-permute-start | bytes 1376264 | tf_op jit(solution)/shard_map/ppermute | solution.py:19
  144.6 10.7 %collective-permute-start.12 = (bf16[448,512]{1,0:T(8,128)(2,1)S(1)}, bf16[448,512]{1,0:T(8,128)(2,1)}, u32[]{:S(2)}, u32[]{:S(2)}) collective-permute-start(bf16[448,512]{1,0:T(8,128)(2,1)S(1)} %collective-permute-done.11), channel_id=1, source_target_pairs={{0,1},{1,2},{2,3},{3,4},{4,5},{5,6},{6,7},{7,8},{8,9},{9,10},{10,1... | collective-permute-start | bytes 1376264 | tf_op jit(solution)/shard_map/ppermute | solution.py:19
  155.3 10.9 %collective-permute-start.13 = (bf16[448,512]{1,0:T(8,128)(2,1)}, bf16[448,512]{1,0:T(8,128)(2,1)}, u32[]{:S(2)}, u32[]{:S(2)}) collective-permute-start(bf16[448,512]{1,0:T(8,128)(2,1)} %collective-permute-done.12), channel_id=1, source_target_pairs={{0,1},{1,2},{2,3},{3,4},{4,5},{5,6},{6,7},{7,8},{8,9},{9,10},{10,1... | collective-permute-start | bytes 1376264 | tf_op jit(solution)/shard_map/ppermute | solution.py:19
  156.2 35.7 %copy-start = (bf16[448,512]{1,0:T(8,128)(2,1)S(1)}, bf16[448,512]{1,0:T(8,128)(2,1)}, u32[]{:S(2)}) copy-start(bf16[448,512]{1,0:T(8,128)(2,1)} %param.13) | copy-start | bytes 1376260
  166.2 10.9 %collective-permute-start.14 = (bf16[448,512]{1,0:T(8,128)(2,1)}, bf16[448,512]{1,0:T(8,128)(2,1)}, u32[]{:S(2)}, u32[]{:S(2)}) collective-permute-start(bf16[448,512]{1,0:T(8,128)(2,1)} %collective-permute-done.13), channel_id=1, source_target_pairs={{0,1},{1,2},{2,3},{3,4},{4,5},{5,6},{6,7},{7,8},{8,9},{9,10},{10,1... | collective-permute-start | bytes 1376264 | tf_op jit(solution)/shard_map/ppermute | solution.py:19
  171.7 24.0 %copy-start.2 = (bf16[448,512]{1,0:T(8,128)(2,1)S(1)}, bf16[448,512]{1,0:T(8,128)(2,1)}, u32[]{:S(2)}) copy-start(bf16[448,512]{1,0:T(8,128)(2,1)} %copy-done.1) | copy-start | bytes 1376260
  172.0 23.1 %copy-start.22 = (bf16[448,512]{1,0:T(8,128)(2,1)S(1)}, bf16[448,512]{1,0:T(8,128)(2,1)}, u32[]{:S(2)}) copy-start(bf16[448,512]{1,0:T(8,128)(2,1)} %copy-done.21) | copy-start | bytes 1376260
  172.0 23.2 %copy-start.20 = (bf16[448,512]{1,0:T(8,128)(2,1)S(1)}, bf16[448,512]{1,0:T(8,128)(2,1)}, u32[]{:S(2)}) copy-start(bf16[448,512]{1,0:T(8,128)(2,1)} %copy-done.19) | copy-start | bytes 1376260
  172.1 23.2 %copy-start.18 = (bf16[448,512]{1,0:T(8,128)(2,1)S(1)}, bf16[448,512]{1,0:T(8,128)(2,1)}, u32[]{:S(2)}) copy-start(bf16[448,512]{1,0:T(8,128)(2,1)} %copy-done.17) | copy-start | bytes 1376260
  172.1 23.2 %copy-start.16 = (bf16[448,512]{1,0:T(8,128)(2,1)S(1)}, bf16[448,512]{1,0:T(8,128)(2,1)}, u32[]{:S(2)}) copy-start(bf16[448,512]{1,0:T(8,128)(2,1)} %copy-done.15) | copy-start | bytes 1376260
  172.1 23.3 %copy-start.14 = (bf16[448,512]{1,0:T(8,128)(2,1)S(1)}, bf16[448,512]{1,0:T(8,128)(2,1)}, u32[]{:S(2)}) copy-start(bf16[448,512]{1,0:T(8,128)(2,1)} %copy-done.13) | copy-start | bytes 1376260
  172.1 23.3 %copy-start.12 = (bf16[448,512]{1,0:T(8,128)(2,1)S(1)}, bf16[448,512]{1,0:T(8,128)(2,1)}, u32[]{:S(2)}) copy-start(bf16[448,512]{1,0:T(8,128)(2,1)} %copy-done.11) | copy-start | bytes 1376260
  172.1 23.4 %copy-start.10 = (bf16[448,512]{1,0:T(8,128)(2,1)S(1)}, bf16[448,512]{1,0:T(8,128)(2,1)}, u32[]{:S(2)}) copy-start(bf16[448,512]{1,0:T(8,128)(2,1)} %copy-done.9) | copy-start | bytes 1376260
  172.1 23.4 %copy-start.8 = (bf16[448,512]{1,0:T(8,128)(2,1)S(1)}, bf16[448,512]{1,0:T(8,128)(2,1)}, u32[]{:S(2)}) copy-start(bf16[448,512]{1,0:T(8,128)(2,1)} %copy-done.7) | copy-start | bytes 1376260
  172.1 23.4 %copy-start.6 = (bf16[448,512]{1,0:T(8,128)(2,1)S(1)}, bf16[448,512]{1,0:T(8,128)(2,1)}, u32[]{:S(2)}) copy-start(bf16[448,512]{1,0:T(8,128)(2,1)} %copy-done.5) | copy-start | bytes 1376260
  172.1 23.5 %copy-start.4 = (bf16[448,512]{1,0:T(8,128)(2,1)S(1)}, bf16[448,512]{1,0:T(8,128)(2,1)}, u32[]{:S(2)}) copy-start(bf16[448,512]{1,0:T(8,128)(2,1)} %copy-done.3) | copy-start | bytes 1376260
  198.6 11.4 %all-to-all-start.1 = ((f32[16,4,512]{2,1,0:T(4,128)}), f32[16,4,512]{2,1,0:T(4,128)S(1)}, u32[]{:S(2)}, u32[]{:S(2)}) async-start(f32[16,4,512]{2,1,0:T(4,128)} %copy.27), calls=%async_computation.1 | async-start | bytes 262144 | tf_op jit(solution)/shard_map/all_to_all | solution.py:71
  (9 other events, 63.3 us)
